TPU v7x, 32 devices: a whole 2x2x4 slice. The times are simulated.
32 devices in a mesh: ea: 4 (over y, x), ha: 8 (over z, core).
Axes of the slice: x: 2, y: 2, z: 4, core: 2. Of those that a mesh axis runs over, the one named last changes fastest.
Arguments:
- tokens: bfloat16 [768, 13312], P('ea', 'ha'), may hold values from -6 to 6
- image_counts: int32 [128], P('ha'), may hold values from 40 to 98, as said below
- kept_patches: int32 [128, 98], P('ha'), may hold values from 0 to 195, as said below
- norm1_gain: bfloat16 [768], P('ea'), may hold values from 0.25 to 1.75
- norm1_bias: bfloat16 [768], P('ea'), may hold values from -3 to 3
- qkv_weight: bfloat16 [768, 2304], P('ea', 'ha'), may hold values from -0.21875 to 0.21875
- query_bias: bfloat16 [768], P('ea'), may hold values from -3 to 3
- value_bias: bfloat16 [768], P('ea'), may hold values from -3 to 3
- out_weight: bfloat16 [768, 768], P('ea', 'ha'), may hold values from -0.625 to 0.625
- out_bias: bfloat16 [768], P('ea'), may hold values from -1.75 to 1.75
- norm2_gain: bfloat16 [768], P('ea'), may hold values from 0.25 to 1.75
- norm2_bias: bfloat16 [768], P('ea'), may hold values from -3 to 3
- in_weight: bfloat16 [768, 3072], P('ea', 'ha'), may hold values from -0.21875 to 0.21875
- in_bias: bfloat16 [3072], P('ha'), may hold values from -3 to 3
- back_weight: bfloat16 [3072, 768], P('ha', 'ea'), may hold values from -0.109375 to 0.109375
- back_bias: bfloat16 [768], P('ea'), may hold values from -1.75 to 1.75
- cotangent: bfloat16 [768, 13312], P('ea', 'ha'), may hold values from -6 to 6
Outputs:
- output: bfloat16 [768, 13312], P('ea', 'ha')
- grad_tokens: float32 [768, 13312], P('ea', 'ha')
- grad_norm1_gain: float32 [768], P('ea')
- grad_norm1_bias: float32 [768], P('ea')
- grad_qkv_weight: float32 [768, 2304], P('ea', 'ha')
- grad_query_bias: float32 [768], P('ea')
- grad_value_bias: float32 [768], P('ea')
- grad_out_weight: float32 [768, 768], P('ea', 'ha')
- grad_out_bias: float32 [768], P('ea')
- grad_norm2_gain: float32 [768], P('ea')
- grad_norm2_bias: float32 [768], P('ea')
- grad_in_weight: float32 [768, 3072], P('ea', 'ha')
- grad_in_bias: float32 [3072], P('ha')
- grad_back_weight: float32 [3072, 768], P('ha', 'ea')
- grad_back_bias: float32 [768], P('ea')
Inputs may be any that keep to these rules, and one draw needn't show every extreme that they name: `image_counts`: each image has between 40 and 98 visible patches; some image has exactly 98 and some exactly 40. `kept_patches`: each row lists distinct patch numbers of its image; only its first image_counts entries are used, in packing order.
All inputs are finite; a program needn't handle non-finite values.
Results may differ from a plain program's by a relative error of at most 0.017.
Values may be sent and summed in bfloat16 or wider, within the bound.
No kernel may reach another device: no remote copies, remote signals or barrier semaphores. Data moves between devices by JAX's collectives and lax.ppermute only.
A program may use at most 192 MiB of HBM per device.

v0:
```python
from functools import partial

import jax
import jax.numpy as jnp
from jax import lax
from jax.sharding import PartitionSpec as P

HEAD_DIM = 64
FF = 3072
GRID = 14


EPSILON = 1e-06
NEGATIVE = -1e30
OVER_ROWS = (((0,), (0,)), ((), ()))
OVER_COLUMNS = (((1,), (1,)), ((), ()))


def positions(patch_index, full_width):
    quarter = full_width // 4
    omega = 1.0 / 10000.0 ** (jnp.arange(quarter, dtype=jnp.float32) / quarter)
    row_part = (patch_index // GRID).astype(jnp.float32)[:, None] * omega[None, :]
    col_part = (patch_index % GRID).astype(jnp.float32)[:, None] * omega[None, :]
    return jnp.concatenate(
        [jnp.sin(row_part), jnp.cos(row_part), jnp.sin(col_part), jnp.cos(col_part)], 1
    )


def layout(image_counts, kept_patches, row_count, full_width):
    image_total, slot_count = kept_patches.shape
    image_ends = jnp.cumsum(image_counts)
    image_starts = image_ends - image_counts
    row_ids = jnp.arange(row_count, dtype=jnp.int32)
    segment = jnp.sum((row_ids[:, None] >= image_ends[None, :]).astype(jnp.int32), 1)
    live_rows = (row_ids < image_ends[image_total - 1]).astype(jnp.float32)
    clipped = jnp.minimum(segment, image_total - 1)
    onehot = (clipped[:, None] == jnp.arange(image_total, dtype=jnp.int32)[None, :]).astype(
        jnp.int32
    )
    first_row = jnp.sum(onehot * image_starts[None, :], 1)
    within = jnp.clip(row_ids - first_row, 0, slot_count - 1)
    patch_index = jnp.take(kept_patches.reshape(-1), clipped * slot_count + within)
    return (segment, live_rows, positions(patch_index, full_width))


def row_totals(first_term, second_term):
    return lax.psum((jnp.sum(first_term, 1), jnp.sum(second_term, 1)), "ea")


def normalize(values, gain, shift, full_width):
    total, squares = row_totals(values, values * values)
    center = total / full_width
    spread = squares / full_width - center * center
    factor = lax.rsqrt(spread + EPSILON)
    centred = (values - center[:, None]) * factor[:, None]
    return (centred * gain + shift, centred, factor)


def normalize_back(grad_normed, centred, factor, gain, full_width):
    scaled = grad_normed * gain
    total, across = row_totals(scaled, scaled * centred)
    return factor[:, None] * (
        scaled - total[:, None] / full_width - centred * (across[:, None] / full_width)
    )


def column_parts(values, weight):
    return lax.psum_scatter(
        jnp.dot(values, weight, preferred_element_type=jnp.float32),
        "ea",
        scatter_dimension=1,
        tiled=True,
    )


def gather_grads(values):
    return lax.all_gather(values, "ea", axis=1, tiled=True)


def head_scores(query, key_rows, same_image, factor):
    scores = (
        lax.dot_general(query, key_rows, OVER_COLUMNS, preferred_element_type=jnp.float32) * factor
    )
    return jnp.where(same_image, scores, NEGATIVE)


def shards(
    tokens,
    image_counts,
    kept_patches,
    norm1_gain,
    norm1_bias,
    qkv_weight,
    query_bias,
    value_bias,
    out_weight,
    out_bias,
    norm2_gain,
    norm2_bias,
    in_weight,
    in_bias,
    back_weight,
    back_bias,
    cotangent,
):
    groups = lax.axis_size("ea")
    column_block = lax.axis_index("ea")
    narrow, row_count = tokens.shape
    full_width = narrow * groups
    heads_here = narrow // HEAD_DIM
    hidden_part = FF // groups
    factor_qk = HEAD_DIM ** (-0.5)
    segment, live_rows, placed = layout(image_counts, kept_patches, row_count, full_width)
    block_start = tokens.T.astype(jnp.float32) + lax.dynamic_slice_in_dim(
        placed, column_block * narrow, narrow, 1
    )
    gain_one = norm1_gain.astype(jnp.float32)
    gain_two = norm2_gain.astype(jnp.float32)
    normed_one, centred_one, factor_one = normalize(
        block_start, gain_one, norm1_bias.astype(jnp.float32), full_width
    )
    first_normed = normed_one.astype(jnp.bfloat16)
    qkv_all, out_all, in_all, back_all, bias_all = (
        lax.all_gather(qkv_weight, "ha", axis=1, tiled=True),
        lax.all_gather(out_weight, "ha", axis=1, tiled=True),
        lax.all_gather(in_weight, "ha", axis=1, tiled=True),
        lax.all_gather(back_weight.T, "ha", axis=1, tiled=True),
        lax.all_gather(in_bias[None, :], "ha", axis=1, tiled=True),
    )
    joined = column_parts(first_normed, qkv_all)
    joined = joined.reshape(row_count, heads_here, 3, HEAD_DIM)
    qkv_shift = jnp.stack(
        [
            query_bias.astype(jnp.float32).reshape(heads_here, HEAD_DIM),
            jnp.zeros((heads_here, HEAD_DIM), jnp.float32),
            value_bias.astype(jnp.float32).reshape(heads_here, HEAD_DIM),
        ],
        1,
    )
    joined = (joined + qkv_shift).astype(jnp.bfloat16)
    same_image = segment[:, None] == segment[None, :]
    mixed_heads = []
    totals = []
    for head_index in range(heads_here):
        scores = head_scores(
            joined[:, head_index, 0], joined[:, head_index, 1], same_image, factor_qk
        )
        peak_score = jnp.max(scores, 1, keepdims=True)
        logsum = peak_score + jnp.log(jnp.sum(jnp.exp(scores - peak_score), 1, keepdims=True))
        probabilities = jnp.exp(scores - logsum).astype(jnp.bfloat16)
        mixed_heads.append(
            jnp.dot(probabilities, joined[:, head_index, 2], preferred_element_type=jnp.float32)
        )
        totals.append(logsum)
    mixed_rows = jnp.concatenate(mixed_heads, 1).astype(jnp.bfloat16)
    attn_out = column_parts(mixed_rows, out_all)
    middle = block_start + attn_out + out_bias.astype(jnp.float32)
    normed_two, centred_two, factor_two = normalize(
        middle, gain_two, norm2_bias.astype(jnp.float32), full_width
    )
    second_normed = normed_two.astype(jnp.bfloat16)
    bias_cols = lax.dynamic_slice_in_dim(
        bias_all[0], column_block * hidden_part, hidden_part, 0
    ).astype(jnp.float32)
    hidden = (
        lax.psum_scatter(
            jnp.dot(second_normed, in_all, preferred_element_type=jnp.float32).astype(jnp.bfloat16),
            "ea",
            scatter_dimension=1,
            tiled=True,
        ).astype(jnp.float32)
        + bias_cols
    )
    activated, gelu_pull = jax.vjp(partial(jax.nn.gelu, approximate=False), hidden)
    active_full = lax.all_gather(activated.astype(jnp.bfloat16), "ea", axis=1, tiled=True)
    feed_out = lax.dot_general(
        active_full, back_all, OVER_COLUMNS, preferred_element_type=jnp.float32
    )
    output = ((middle + feed_out + back_bias.astype(jnp.float32)) * live_rows[:, None]).astype(
        jnp.bfloat16
    )
    grad_out = cotangent.T.astype(jnp.float32) * live_rows[:, None]
    grad_out_low = grad_out.astype(jnp.bfloat16)
    grad_back_t = lax.dot_general(
        grad_out_low, active_full, OVER_ROWS, preferred_element_type=jnp.float32
    )
    grad_active = lax.psum_scatter(
        jnp.dot(grad_out_low, back_all, preferred_element_type=jnp.float32).astype(jnp.bfloat16),
        "ea",
        scatter_dimension=1,
        tiled=True,
    ).astype(jnp.float32)
    (grad_hidden,) = gelu_pull(grad_active)
    grad_hidden_low = grad_hidden.astype(jnp.bfloat16)
    grad_hidden_full = lax.all_gather(grad_hidden_low, "ea", axis=1, tiled=True)
    grad_in_w = lax.dot_general(
        second_normed, grad_hidden_full, OVER_ROWS, preferred_element_type=jnp.float32
    )
    grad_second = lax.dot_general(
        grad_hidden_full, in_all, OVER_COLUMNS, preferred_element_type=jnp.float32
    )
    grad_hidden_bias = jnp.sum(grad_hidden_full.astype(jnp.float32), 0)[None, :]
    grad_middle = grad_out + normalize_back(
        grad_second, centred_two, factor_two, gain_two, full_width
    )
    grad_middle_low = grad_middle.astype(jnp.bfloat16)
    grad_attn_full = gather_grads(grad_middle_low)
    grad_out_w = lax.dot_general(
        mixed_rows, grad_attn_full, OVER_ROWS, preferred_element_type=jnp.float32
    )
    grad_mixed = lax.dot_general(
        grad_attn_full, out_all, OVER_COLUMNS, preferred_element_type=jnp.float32
    ).astype(jnp.bfloat16)
    head_grads = []
    for head_index in range(heads_here):
        query = joined[:, head_index, 0]
        key_rows = joined[:, head_index, 1]
        value_rows = joined[:, head_index, 2]
        scores = head_scores(query, key_rows, same_image, factor_qk)
        probabilities = jnp.exp(scores - totals[head_index])
        grad_head = grad_mixed[:, head_index * HEAD_DIM : (head_index + 1) * HEAD_DIM]
        grad_prob = lax.dot_general(
            grad_head, value_rows, OVER_COLUMNS, preferred_element_type=jnp.float32
        )
        grad_score = (
            probabilities * (grad_prob - jnp.sum(probabilities * grad_prob, 1, keepdims=True))
        ).astype(jnp.bfloat16)
        grad_query = jnp.dot(grad_score, key_rows, preferred_element_type=jnp.float32) * factor_qk
        grad_keys = (
            lax.dot_general(grad_score, query, OVER_ROWS, preferred_element_type=jnp.float32)
            * factor_qk
        )
        grad_values = lax.dot_general(
            probabilities.astype(jnp.bfloat16),
            grad_head,
            OVER_ROWS,
            preferred_element_type=jnp.float32,
        )
        head_grads.append(jnp.stack([grad_query, grad_keys, grad_values], 1))
    grad_joined = jnp.stack(head_grads, 1).astype(jnp.bfloat16)
    grad_query_bias = jnp.sum(grad_joined[:, :, 0].astype(jnp.float32), 0).reshape(-1)
    grad_value_bias = jnp.sum(grad_joined[:, :, 2].astype(jnp.float32), 0).reshape(-1)
    grad_flat = grad_joined.reshape(row_count, 3 * narrow)
    grad_qkv_full = gather_grads(grad_flat)
    grad_qkv_w = lax.dot_general(
        first_normed, grad_qkv_full, OVER_ROWS, preferred_element_type=jnp.float32
    )
    grad_first = lax.dot_general(
        grad_qkv_full, qkv_all, OVER_COLUMNS, preferred_element_type=jnp.float32
    )
    grad_tokens = grad_middle + normalize_back(
        grad_first, centred_one, factor_one, gain_one, full_width
    )
    summed = lax.psum(
        (
            jnp.sum(grad_first * centred_one, 0),
            jnp.sum(grad_first, 0),
            grad_query_bias,
            grad_value_bias,
            jnp.sum(grad_middle_low.astype(jnp.float32), 0),
            jnp.sum(grad_second * centred_two, 0),
            jnp.sum(grad_second, 0),
            jnp.sum(grad_out, 0),
        ),
        "ha",
    )
    scattered = (
        lax.psum_scatter(grad_qkv_w, "ha", scatter_dimension=1, tiled=True),
        lax.psum_scatter(grad_out_w, "ha", scatter_dimension=1, tiled=True),
        lax.psum_scatter(grad_in_w, "ha", scatter_dimension=1, tiled=True),
        lax.psum_scatter(grad_back_t, "ha", scatter_dimension=1, tiled=True),
        lax.psum_scatter(grad_hidden_bias, "ha", scatter_dimension=1, tiled=True),
    )
    return (
        output.T,
        grad_tokens.T,
        summed[0],
        summed[1],
        scattered[0],
        summed[2],
        summed[3],
        scattered[1],
        summed[4],
        summed[5],
        summed[6],
        scattered[2],
        scattered[4][0],
        scattered[3].T,
        summed[7],
    )


def solution(mesh):
    return jax.shard_map(
        shards,
        mesh=mesh,
        in_specs=(
            P("ea", "ha"),
            P("ha"),
            P("ha", None),
            P("ea"),
            P("ea"),
            P("ea", "ha"),
            P("ea"),
            P("ea"),
            P("ea", "ha"),
            P("ea"),
            P("ea"),
            P("ea"),
            P("ea", "ha"),
            P("ha"),
            P("ha", "ea"),
            P("ea"),
            P("ea", "ha"),
        ),
        out_specs=(
            P("ea", "ha"),
            P("ea", "ha"),
            P("ea"),
            P("ea"),
            P("ea", "ha"),
            P("ea"),
            P("ea"),
            P("ea", "ha"),
            P("ea"),
            P("ea"),
            P("ea"),
            P("ea", "ha"),
            P("ha"),
            P("ha", "ea"),
            P("ea"),
        ),
        check_vma=False,
    )
```

profile of v0, /device:TPU:0, one launch (start us, length us, event | category | flops | bytes accessed | tf_op | source)
XLA Modules:
  0.0 1057.4 jit_solution(10966846678042547708)
XLA Ops:
  12.0 9.1 gather_fusion
  21.3 19.3 %all_gather.27 = bf16[192,2304]{0,1:T(8,128)(2,1)S(1)} all-gather(bf16[192,288]{0,1:T(8,128)(2,1)S(1)} %copy.38), channel_id=1, replica_groups=mesh['ea'=4,'ha'=8] {'ha'}, dimensions={1}, use_global_device_ids=true | all-gather | bytes 995328 | tf_op jit(solution)/shard_map/all_gather | solution.py:124
  40.6 8.9 multiply_sine_fusion.1
  50.4 27.8 %all-reduce.4 = (f32[1664]{0:T(1024)S(1)}, f32[1664]{0:T(1024)S(1)}) all-reduce(f32[1664]{0:T(1024)S(1)} %get-tuple-element.28, f32[1664]{0:T(1024)S(1)} %get-tuple-element.27), channel_id=1, replica_groups=mesh['ea'=4,'ha'=8] {'ea'}, use_global_device_ids=true, to_apply=%region_6.7 | all-reduce | flops 3328 | bytes 26624 | tf_op jit(solution)/shard_map/psum | solution.py:47
  78.8 7.8 fusion.62
  87.6 16.2 %all_gather.28 = bf16[192,768]{0,1:T(8,128)(2,1)} all-gather(bf16[192,96]{0,1:T(8,128)(2,1)S(1)} %copy.39), channel_id=1, replica_groups=mesh['ea'=4,'ha'=8] {'ha'}, dimensions={1}, use_global_device_ids=true | all-gather | bytes 331776 | tf_op jit(solution)/shard_map/all_gather | solution.py:125
  103.9 125.4 %reduce-scatter.16.cloned.1.call-done = f32[1664,576]{0,1:T(8,128)} async-done(((f32[1664,2304]{0,1:T(8,128)}), f32[1664,576]{0,1:T(8,128)}) %reduce-scatter.16.cloned.1.call-update) | async-done | bytes 3833872 | tf_op jit(solution)/shard_map/reduce_scatter | solution.py:68
  229.3 2.4 add_convert_fusion
  231.7 5.4 fusion.69
  237.1 2.0 fusion.70
  239.2 2.0 fusion.71
  241.2 11.2 %exponential_reduce_fusion = f32[1664]{0:T(1024)S(1)} fusion(f32[1664,1664]{0,1:T(8,128)} %get-tuple-element.66, f32[1664]{0:T(1024)S(1)} %get-tuple-element.65), kind=kLoop, calls=%fused_computation.14 | loop fusion | flops 5536128 | bytes 11088896 | tf_op jit(solution)/shard_map/reduce_sum | solution.py:149
  254.0 1.6 exponential_reduce_fusion.2
  255.6 6.1 convolution_convert_fusion.3
  261.7 3.3 convolution_convert_fusion.4
  265.0 2.9 convolution_convert_fusion.5
  268.7 3.2 fusion.44
  273.8 8.4 convolution_convert_fusion
  282.9 49.5 %reduce-scatter.18.cloned.1.call-done = f32[1664,192]{0,1:T(8,128)} async-done(((f32[1664,768]{0,1:T(8,128)}), f32[1664,192]{0,1:T(8,128)}) %reduce-scatter.18.cloned.1.call-update) | async-done | bytes 1277968 | tf_op jit(solution)/shard_map/reduce_scatter | solution.py:68
  334.0 15.3 %all-reduce.3 = (f32[1664]{0:T(1024)S(1)}, f32[1664]{0:T(1024)S(1)}) all-reduce(f32[1664]{0:T(1024)S(1)} %get-tuple-element.26, f32[1664]{0:T(1024)S(1)} %get-tuple-element.25), channel_id=1, replica_groups=mesh['ea'=4,'ha'=8] {'ea'}, use_global_device_ids=true, to_apply=%region_18.19 | all-reduce | flops 3328 | bytes 26624 | tf_op jit(solution)/shard_map/psum | solution.py:47
  349.4 8.2 convolution_convert_fusion.1
  358.2 12.7 %all-gather.1 = bf16[8,1,384]{2,1,0:T(2,128)(2,1)S(1)} all-gather(bf16[1,1,384]{2,1,0:T(2,128)(2,1)S(1)} %reshape.222), channel_id=2, replica_groups=mesh['ea'=4,'ha'=8] {'ha'}, dimensions={0}, use_global_device_ids=true | all-gather | bytes 6912 | tf_op jit(solution)/shard_map/all_gather | solution.py:128
  371.0 66.0 %reduce-scatter.22.cloned.1.call-done = bf16[1664,768]{1,0:T(8,128)(2,1)} async-done(((bf16[1664,3072]{1,0:T(8,128)(2,1)}), bf16[1664,768]{1,0:T(8,128)(2,1)}) %reduce-scatter.22.cloned.1.call-update) | async-done | bytes 2555920 | tf_op jit(solution)/shard_map/reduce_scatter | solution.py:187
  437.0 104.4 %reduce-scatter.20.cloned.1.call-done = bf16[1664,768]{1,0:T(8,128)(2,1)} async-done(((bf16[1664,3072]{1,0:T(8,128)(2,1)}), bf16[1664,768]{1,0:T(8,128)(2,1)}) %reduce-scatter.20.cloned.1.call-update) | async-done | bytes 2555920 | tf_op jit(solution)/shard_map/reduce_scatter | solution.py:166
  541.5 14.8 %fusion.8 = (bf16[1664,768]{1,0:T(8,128)(2,1)}, f32[1664,768]{1,0:T(8,128)}) fusion(bf16[1664,768]{1,0:T(8,128)(2,1)} %reduce-scatter.22.cloned.1.call-done, bf16[1664,768]{1,0:T(8,128)(2,1)} %reduce-scatter.20.cloned.1.call-done, f32[768]{0:T(1024)S(1)} %dynamic-slice_convert_fusion), kind=kLoop, calls=%fused_computation.30 | loop fusion | flops 95846400 | bytes 12782592 | tf_op jit(solution)/shard_map/convert_element_type | solution.py:194
  556.5 102.8 %all-gather.15.cloned.1.call-done = bf16[1664,3072]{1,0:T(8,128)(2,1)} async-done(((bf16[1664,768]{1,0:T(8,128)(2,1)}), bf16[1664,3072]{1,0:T(8,128)(2,1)}) %all-gather.15.cloned.1.call-update) | async-done | bytes 10223632 | tf_op jit(solution)/shard_map/all_gather | solution.py:195
  659.3 8.4 multiply_reduce_fusion.3
  667.7 15.1 %all-reduce.2 = (f32[1664]{0:T(1024)S(1)}, f32[1664]{0:T(1024)S(1)}) all-reduce(f32[1664]{0:T(1024)S(1)} %get-tuple-element.16, f32[1664]{0:T(1024)S(1)} %get-tuple-element.22), channel_id=1, replica_groups=mesh['ea'=4,'ha'=8] {'ea'}, use_global_device_ids=true, to_apply=%region_24.25 | all-reduce | flops 3328 | bytes 26624 | tf_op jit(solution)/shard_map/psum | solution.py:47
  682.8 2.0 convert_reduce_fusion.1
  684.8 39.2 %all-gather.17.cloned.1.call-done = bf16[1664,768]{0,1:T(8,128)(2,1)} async-done(((bf16[1664,192]{0,1:T(8,128)(2,1)}), bf16[1664,768]{0,1:T(8,128)(2,1)}) %all-gather.17.cloned.1.call-update) | async-done | bytes 2555920 | tf_op jit(solution)/shard_map/all_gather | solution.py:77
  724.0 2.7 convolution_convert_fusion.2
  726.7 6.9 convolution_bitcast_fusion.3
  733.7 2.5 convolution_bitcast_fusion.2
  736.5 2.5 convolution_bitcast_fusion.1
  739.0 3.3 multiply_reduce_fusion
  742.3 4.1 multiply_convert_fusion
  746.5 4.5 fusion.28
  750.9 2.0 fusion.31
  753.0 3.8 multiply_reduce_fusion.1
  756.8 4.8 multiply_convert_fusion.1
  761.5 5.1 fusion.27
  766.7 2.0 fusion.30
  768.7 3.2 multiply_reduce_fusion.2
  771.9 2.1 multiply_convert_fusion.2
  774.1 2.7 fusion.26
  776.8 2.1 fusion.29
  781.2 4.6 multiply_convert_fusion.3
  786.0 7.2 convert_reduce_fusion
  793.2 1.7 copy.44
  795.0 3.5 convolution_bitcast_fusion.4
  798.6 63.9 %all-gather.19.cloned.1.call-done = bf16[1664,2304]{0,1:T(8,128)(2,1)} async-done(((bf16[1664,576]{0,1:T(8,128)(2,1)}), bf16[1664,2304]{0,1:T(8,128)(2,1)}) %all-gather.19.cloned.1.call-update) | async-done | bytes 7667728 | tf_op jit(solution)/shard_map/all_gather | solution.py:77
  862.6 7.0 convolution_bitcast_fusion
  869.7 97.6 %all-gather.11.cloned.1.call-done = bf16[1664,3072]{1,0:T(8,128)(2,1)} async-done(((bf16[1664,768]{1,0:T(8,128)(2,1)}), bf16[1664,3072]{1,0:T(8,128)(2,1)}) %all-gather.11.cloned.1.call-update) | async-done | bytes 10223632 | tf_op jit(solution)/shard_map/all_gather | solution.py:175
  967.3 7.6 fusion.43
  975.2 7.7 fusion.63
  983.2 8.6 fusion.25
  991.8 1.7 bitcast_reduce_fusion
  995.2 1.6 copy.43
  996.8 6.7 multiply_reduce_fusion.4
  1003.5 17.2 %all-reduce = (f32[192]{0:T(256)}, f32[192]{0:T(256)}, f32[192]{0:T(256)}, f32[192]{0:T(256)}, f32[192]{0:T(256)}, /*index=5*/f32[192]{0:T(256)}, f32[192]{0:T(256)}, f32[192]{0:T(256)}) all-reduce(f32[192]{0:T(256)S(1)} %get-tuple-element.17, f32[192]{0:T(256)S(1)} %get-tuple-element.24, ...), channel_id=1, replica_groups=mesh['ea'=4,'ha'=8] {'ha'}, use_global_device_ids=true, to_apply=%region_33.34 | all-reduce | flops 1536 | bytes 12288 | tf_op jit(solution)/shard_map/psum | solution.py:254
  1020.8 15.1 %all-reduce.1 = (f32[1664]{0:T(1024)S(1)}, f32[1664]{0:T(1024)S(1)}) all-reduce(f32[1664]{0:T(1024)S(1)} %get-tuple-element.18, f32[1664]{0:T(1024)S(1)} %get-tuple-element.21), channel_id=1, replica_groups=mesh['ea'=4,'ha'=8] {'ea'}, use_global_device_ids=true, to_apply=%region_31.32 | all-reduce | flops 3328 | bytes 26624 | tf_op jit(solution)/shard_map/psum | solution.py:47
  1035.8 3.6 add_bitcast_fusion
  1039.4 1.8 copy.41
  1041.2 8.5 reduce-scatter.24.cloned.1.call-done
  (216 shorter events, 19.2 us)
Async XLA Ops:
  8.0 13.2 %copy-start.29 = (bf16[192,288]{1,0:T(8,128)(2,1)S(1)}, bf16[192,288]{1,0:T(8,128)(2,1)}, u32[]{:S(2)}) copy-start(bf16[192,288]{1,0:T(8,128)(2,1)} %param.22) | copy-start | bytes 331780
  8.0 221.3 %reduce-scatter.16.cloned.1.call-start = ((), (), s32[]{:S(2)}) async-start(), calls=%async_computation.9 | async-start | bytes 19169280 | tf_op jit(solution)/shard_map/reduce_scatter | solution.py:68
  10.4 67.8 %copy-start.39 = (f32[192]{0:T(256)}, f32[192]{0:T(256)S(1)}, u32[]{:S(2)}) copy-start(f32[192]{0:T(256)S(1)} %convert_element_type.144) | copy-start | bytes 2308
  11.1 67.2 %copy-start.44 = (f32[192]{0:T(256)}, f32[192]{0:T(256)S(1)}, u32[]{:S(2)}) copy-start(f32[192]{0:T(256)S(1)} %convert_element_type.145) | copy-start | bytes 2308
  21.1 28.4 %copy-start.28 = (bf16[192,1664]{1,0:T(8,128)(2,1)S(1)}, bf16[192,1664]{1,0:T(8,128)(2,1)}, u32[]{:S(2)}) copy-start(bf16[192,1664]{1,0:T(8,128)(2,1)} %param.17) | copy-start | bytes 1916932
  40.6 37.6 %copy-start.13 = (bf16[192,2304]{0,1:T(8,128)(2,1)}, bf16[192,2304]{0,1:T(8,128)(2,1)S(1)}, u32[]{:S(2)}) copy-start(bf16[192,2304]{0,1:T(8,128)(2,1)S(1)} %all_gather.27) | copy-start | bytes 2654212
  50.4 36.2 %copy-start.6 = (f32[1664,192]{0,1:T(8,128)}, f32[1664,192]{0,1:T(8,128)S(1)}, u32[]{:S(2)}) copy-start(f32[1664,192]{0,1:T(8,128)S(1)} %get-tuple-element.50) | copy-start | bytes 3833860
  86.7 187.1 %all-gather.13.cloned.1.call-start = ((), (), s32[]{:S(2)}) async-start(), calls=%async_computation.14 | async-start | bytes 1327104 | tf_op jit(solution)/shard_map/all_gather | solution.py:127
  87.2 245.1 %reduce-scatter.18.cloned.1.call-start = ((), (), s32[]{:S(2)}) async-start(), calls=%async_computation.10 | async-start | bytes 6389760 | tf_op jit(solution)/shard_map/reduce_scatter | solution.py:68
  231.7 7.4 copy-start.11
  239.1 22.6 %copy-start.1 = (f32[1664,1664]{0,1:T(8,128)}, f32[1664,1664]{0,1:T(8,128)S(1)}, u32[]{:S(2)}) copy-start(f32[1664,1664]{0,1:T(8,128)S(1)} %get-tuple-element.68) | copy-start | bytes 33226756
  241.2 23.8 %copy-start = (f32[1664,1664]{0,1:T(8,128)}, f32[1664,1664]{0,1:T(8,128)S(1)}, u32[]{:S(2)}) copy-start(f32[1664,1664]{0,1:T(8,128)S(1)} %get-tuple-element.70) | copy-start | bytes 33226756
  261.7 6.2 copy-start.19
  265.0 2.9 copy-start.21
  265.0 3.6 copy-start.18
  268.7 5.1 copy-start.9
  271.9 77.4 %all-gather.9.cloned.1.call-start = ((), (), s32[]{:S(2)}) async-start(), calls=%async_computation.11 | async-start | bytes 1327104 | tf_op jit(solution)/shard_map/all_gather | solution.py:126
  272.5 164.5 %reduce-scatter.22.cloned.1.call-start = ((), (), s32[]{:S(2)}) async-start(), calls=%async_computation.15 | async-start | bytes 12779520 | tf_op jit(solution)/shard_map/reduce_scatter | solution.py:187
  282.2 50.2 %copy-start.7 = (f32[1664,192]{0,1:T(8,128)S(1)}, f32[1664,192]{0,1:T(8,128)}, u32[]{:S(2)}) copy-start(f32[1664,192]{0,1:T(8,128)} %copy-done.6) | copy-start | bytes 3833860
  282.2 259.3 %reduce-scatter.20.cloned.1.call-start = ((), (), s32[]{:S(2)}) async-start(), calls=%async_computation.12 | async-start | bytes 12779520 | tf_op jit(solution)/shard_map/reduce_scatter | solution.py:166
  282.8 400.0 %copy-start.37 = (f32[192]{0:T(256)}, f32[192]{0:T(256)S(1)}, u32[]{:S(2)}) copy-start(f32[192]{0:T(256)S(1)} %convert_element_type.152) | copy-start | bytes 2308
  282.8 74.7 %copy-start.41 = (f32[192]{0:T(256)}, f32[192]{0:T(256)S(1)}, u32[]{:S(2)}) copy-start(f32[192]{0:T(256)S(1)} %convert_element_type.153) | copy-start | bytes 2308
  334.0 348.8 %copy-start.4 = (f32[1664,192]{0,1:T(8,128)}, f32[1664,192]{0,1:T(8,128)S(1)}, u32[]{:S(2)}) copy-start(f32[1664,192]{0,1:T(8,128)S(1)} %get-tuple-element.49) | copy-start | bytes 3833860
  357.6 301.7 %all-gather.15.cloned.1.call-start = ((), (), s32[]{:S(2)}) async-start(), calls=%async_computation.16 | async-start | bytes 12779520 | tf_op jit(solution)/shard_map/all_gather | solution.py:195
  371.0 185.2 %copy-start.35 = (f32[768]{0:T(1024)}, f32[768]{0:T(1024)S(1)}, u32[]{:S(2)}) copy-start(f32[768]{0:T(1024)S(1)} %dynamic-slice_convert_fusion) | copy-start | bytes 9220
  556.2 167.8 %all-gather.17.cloned.1.call-start = ((), (), s32[]{:S(2)}) async-start(), calls=%async_computation.17 | async-start | bytes 3194880 | tf_op jit(solution)/shard_map/all_gather | solution.py:77
  667.7 65.9 %copy-start.17 = (f32[1664,192]{0,1:T(8,128)}, f32[1664,192]{0,1:T(8,128)S(1)}, u32[]{:S(2)}) copy-start(f32[1664,192]{0,1:T(8,128)S(1)} %get-tuple-element.71) | copy-start | bytes 3833860
  684.8 177.8 %all-gather.19.cloned.1.call-start = ((), (), s32[]{:S(2)}) async-start(), calls=%async_computation.18 | async-start | bytes 9584640 | tf_op jit(solution)/shard_map/all_gather | solution.py:77
  724.0 9.6 slice-start.3
  726.7 9.5 copy-start.14
  726.7 7.0 slice-start.4
  726.7 7.0 slice-start.5
  726.7 9.5 slice-start.6
  726.7 9.5 slice-start.7
  746.5 4.5 copy-start.2
  746.5 6.5 copy-start.15
  756.8 11.9 %slice-start = ((s8[11075584]{0:T(1024)(128)(4,1)}), s8[4194304]{0:T(1024)(128)(4,1)S(1)}, s32[]{:S(2)}) async-start(s8[11075584]{0:T(1024)(128)(4,1)} %bitcast.134), calls=%async_computation.24 | async-start | bytes 8388608
  756.8 11.9 %slice-start.1 = ((s8[11075584]{0:T(1024)(128)(4,1)}), s8[4194304]{0:T(1024)(128)(4,1)S(1)}, s32[]{:S(2)}) async-start(s8[11075584]{0:T(1024)(128)(4,1)} %bitcast.134), calls=%async_computation.25 | async-start | bytes 8388608
  756.8 11.9 %slice-start.2 = ((s8[11075584]{0:T(1024)(128)(4,1)}), s8[2686976]{0:T(1024)(128)(4,1)S(1)}, s32[]{:S(2)}) async-start(s8[11075584]{0:T(1024)(128)(4,1)} %bitcast.134), calls=%async_computation.26 | async-start | bytes 5373952
  761.5 5.1 copy-start.3
  761.5 7.2 copy-start.16
  774.1 4.9 copy-start.27
  780.8 186.5 %all-gather.11.cloned.1.call-start = ((), (), s32[]{:S(2)}) async-start(), calls=%async_computation.13 | async-start | bytes 12779520 | tf_op jit(solution)/shard_map/all_gather | solution.py:175
  785.9 9.1 copy-start.20
  785.9 9.1 copy-start.22
  785.9 9.1 copy-start.24
  785.9 205.9 %reduce-scatter.32.cloned.1.call-start = ((), (), s32[]{:S(2)}) async-start(), calls=%async_computation.23 | async-start | bytes 1769472
  793.2 69.3 %copy-start.8 = (f32[1664,192]{0,1:T(8,128)S(1)}, f32[1664,192]{0,1:T(8,128)}, u32[]{:S(2)}) copy-start(f32[1664,192]{0,1:T(8,128)} %copy-done.6) | copy-start | bytes 3833860
  793.2 69.3 %copy-start.31 = (f32[1664]{0:T(1024)S(1)}, f32[1664]{0:T(1024)}, u32[]{:S(2)}) copy-start(f32[1664]{0:T(1024)} %copy-done.30) | copy-start | bytes 19972
  793.2 69.3 %copy-start.33 = (f32[1664]{0:T(1024)S(1)}, f32[1664]{0:T(1024)}, u32[]{:S(2)}) copy-start(f32[1664]{0:T(1024)} %copy-done.32) | copy-start | bytes 19972
  793.2 69.3 %copy-start.40 = (f32[192]{0:T(256)S(1)}, f32[192]{0:T(256)}, u32[]{:S(2)}) copy-start(f32[192]{0:T(256)} %copy-done.39) | copy-start | bytes 2308
  793.2 69.3 %copy-start.45 = (f32[192]{0:T(256)S(1)}, f32[192]{0:T(256)}, u32[]{:S(2)}) copy-start(f32[192]{0:T(256)} %copy-done.44) | copy-start | bytes 2308
  794.9 200.3 %reduce-scatter.30.cloned.1.call-start = ((), (), s32[]{:S(2)}) async-start(), calls=%async_computation.22 | async-start | bytes 884736
  798.5 168.8 %copy-start.10 = (bf16[192,1664]{1,0:T(8,128)(2,1)S(1)}, bf16[192,1664]{1,0:T(8,128)(2,1)}, u32[]{:S(2)}) copy-start(bf16[192,1664]{1,0:T(8,128)(2,1)} %param.33) | copy-start | bytes 1916932
  798.6 240.9 %reduce-scatter.28.cloned.1.call-start = ((), (), s32[]{:S(2)}) async-start(), calls=%async_computation.21 | async-start | bytes 2654208
  869.6 105.6 %copy-start.5 = (f32[1664,192]{0,1:T(8,128)S(1)}, f32[1664,192]{0,1:T(8,128)}, u32[]{:S(2)}) copy-start(f32[1664,192]{0,1:T(8,128)} %copy-done.4) | copy-start | bytes 3833860
  869.6 105.6 %copy-start.38 = (f32[192]{0:T(256)S(1)}, f32[192]{0:T(256)}, u32[]{:S(2)}) copy-start(f32[192]{0:T(256)} %copy-done.37) | copy-start | bytes 2308
  869.6 105.6 %copy-start.42 = (f32[192]{0:T(256)S(1)}, f32[192]{0:T(256)}, u32[]{:S(2)}) copy-start(f32[192]{0:T(256)} %copy-done.41) | copy-start | bytes 2308
  869.6 171.6 %reduce-scatter.26.cloned.1.call-start = ((), (), s32[]{:S(2)}) async-start(), calls=%async_computation.20 | async-start | bytes 2654208 | tf_op jit(solution)/shard_map/reduce_scatter | solution.py:271
  975.0 8.0 copy-start.54
  975.0 74.8 %reduce-scatter.24.cloned.1.call-start = ((), (), s32[]{:S(2)}) async-start(), calls=%async_computation.19 | async-start | bytes 2654208 | tf_op jit(solution)/shard_map/reduce_scatter | solution.py:270
  996.8 6.7 copy-start.43
  996.8 6.7 copy-start.47
  996.8 6.7 copy-start.48
  (15 other events, 18.8 us)
Sparse Core Ops, SparseCore 0:
  86.8 142.5 reduce-scatter.15
  272.0 60.2 reduce-scatter.17
  335.5 101.4 reduce-scatter.21
  440.1 101.3 reduce-scatter.19
  556.4 102.8 all-gather.14
  684.9 39.0 all-gather.16
  780.9 81.5 all-gather.18
  864.4 102.8 all-gather.10
Sparse Core Ops, SparseCore 1:
  88.7 22.9 all-gather.12
  274.0 22.9 all-gather.8
  795.0 33.9 reduce-scatter.31
  831.3 29.5 reduce-scatter.29
  869.7 36.4 reduce-scatter.27
  975.0 36.4 reduce-scatter.25
  1014.3 35.4 reduce-scatter.23
where the time goes:
time: 1060 us
  waiting for transfers between devices  659 us (62%)
  matrix products  142 us (13%)
  blocking collectives  139 us (13%)
  other arithmetic  78 us (7%)
  local copies, waits for them, and re-layouts  21.5 us (2%)
  between operations  16.8 us (2%)
    reduce_scatter x2, waiting for transfers between devices, column_parts(): lax.psum_scatter(jnp.dot(values, weight, preferred_element_type=jnp.float...  175 us
    reduce_scatter x1, waiting for transfers between devices, shards(): lax.psum_scatter(jnp.dot(second_normed, in_all, preferred_element_type=jn...  104 us
    all_gather x2, waiting for transfers between devices, gather_grads(): return lax.all_gather(values, 'ea', axis=1, tiled=True)  103 us
    all_gather x1, waiting for transfers between devices, shards(): grad_hidden_full = lax.all_gather(grad_hidden_low, 'ea', axis=1, tiled=True)  103 us
    all_gather x1, waiting for transfers between devices, shards(): lax.all_gather(activated.astype(jnp.bfloat16), 'ea', axis=1, tiled=True)  97.6 us
    psum x4, blocking collectives, row_totals(): return lax.psum((jnp.sum(first_term, 1), jnp.sum(second_term, 1)), 'ea')  73.3 us
    reduce_scatter x1, waiting for transfers between devices, shards(): lax.psum_scatter(jnp.dot(grad_out_low, back_all, preferred_element_type=j...  66 us
  transfers between devices with their start and end apart: 15, of which 9 were waited for; matrix products, arithmetic and copies ran while one was open for 12% of the time, Pallas kernels for 0%

commit v1 on v0

v1 whole, which is shorter than its diff:
```python
from functools import partial

import jax
import jax.numpy as jnp
from jax import lax
from jax.experimental import pallas as pl
from jax.experimental.pallas import tpu as pltpu
from jax.sharding import PartitionSpec as P

HEAD_DIM = 64
GRID = 14
EPSILON = 1e-06
NEGATIVE = -1e30
BLOCKS = 8
VEC_ROWS = 16
NN = (((1,), (0,)), ((), ()))
NT = (((1,), (1,)), ((), ()))
TN = (((0,), (0,)), ((), ()))
F32 = jnp.float32
BF16 = jnp.bfloat16
SMEM = pl.BlockSpec(memory_space=pltpu.SMEM)
VMEM = pl.BlockSpec(memory_space=pltpu.VMEM)
PARAMS = pltpu.CompilerParams(vmem_limit_bytes=56 * 1024 * 1024)


def dot(a, b, dims):
    return lax.dot_general(a, b, dims, preferred_element_type=F32)


def iota(shape, axis):
    return lax.broadcasted_iota(jnp.int32, shape, axis)


def prefix(counts, starts):
    total = jnp.int32(0)
    for i in range(counts.shape[0]):
        starts[i] = total
        total = total + counts[i]


def select_rows(sel, counts, starts, part, images, rows, window, slots):
    first = starts[part * images]
    base = jnp.minimum(first // 128, (slots - window) // 128) * 128
    base = pl.multiple_of(base, 128)
    row = iota((rows, window), 0)
    gap = iota((rows, window), 1) - row
    for i in range(images):
        image = part * images + i
        hit = (gap == starts[image] - base) & (row < counts[image])
        sel[i * rows : (i + 1) * rows, :] = jnp.where(hit, 1.0, 0.0).astype(BF16)
    return base


def pack_kernel(images, rows, window, meta, counts, tokens, cotangent, x_out, y_out, starts, sel):
    prefix(counts, starts)
    for d in range(x_out.shape[0]):
        base = select_rows(
            sel, counts, starts, meta[0] ^ d, images, rows, window, tokens.shape[1]
        )
        chosen = sel[...]
        x_out[d] = dot(chosen, tokens[:, pl.ds(base, window)], NT).astype(BF16)
        y_out[d] = dot(chosen, cotangent[:, pl.ds(base, window)], NT).astype(BF16)


def unpack_kernel(images, rows, window, meta, counts, *refs):
    parts, (out, starts, sel, total) = refs[:-4], refs[-4:]
    prefix(counts, starts)
    total[...] = jnp.zeros_like(total)
    for d, part in enumerate(parts):
        base = select_rows(sel, counts, starts, meta[0] ^ d, images, rows, window, out.shape[1])
        total[:, pl.ds(base, window)] += dot(part[...], sel[...], TN)
    out[...] = total[...].astype(out.dtype)


def norm_parts(values):
    center = jnp.mean(values, 1, keepdims=True)
    centred = values - center
    factor = lax.rsqrt(jnp.mean(centred * centred, 1, keepdims=True) + EPSILON)
    return centred * factor, factor


def norm_back(grad, xhat, factor, gain):
    scaled = grad * gain
    mean = jnp.mean(scaled, 1, keepdims=True)
    across = jnp.mean(scaled * xhat, 1, keepdims=True)
    return factor * (scaled - mean - xhat * across)


def colsum(values):
    return jnp.sum(values, 0, keepdims=True)


def attend_kernel(images, rows, meta, counts, *refs):
    x_refs, (patches, sines, cosines, g1) = refs[:4], refs[4:8]
    x1_out, x0, h1_out, qkv_out, p_out, o_out, vecs, inb, wq, wo = refs[8:]
    me = meta[0]
    parts = len(x_refs)
    narrow = x_refs[0].shape[1]
    wide = 3 * narrow
    half = wide // 2
    outer = narrow // 2
    heads = narrow // HEAD_DIM
    for d in range(parts):
        low, high = d * narrow, (d + 1) * narrow
        vecs[:, low:high] = g1[(me ^ d) * BLOCKS, narrow:, :narrow].astype(F32)
        for z in range(parts):
            for k in range(2):
                block = g1[(me ^ d) * BLOCKS + 2 * z + k, :narrow, :half]
                wq[z, low:high, k * half : (k + 1) * half] = block
                block = g1[z * BLOCKS + 2 * (me ^ d) + k, :narrow, half:]
                wo[z, :, low + k * outer : low + (k + 1) * outer] = block
    for h in range(BLOCKS):
        inb[h] = g1[h, narrow:, :].astype(F32)[8:9]
    pieces = []
    for d in range(parts):
        e = me ^ d
        table = jnp.where(e % 2 == 0, sines[...], cosines[...])
        high = table.astype(BF16)
        rest = table - high.astype(F32)
        middle = rest.astype(BF16)
        low = (rest - middle.astype(F32)).astype(BF16)
        stacked = jnp.concatenate([high, middle, low], 0)
        depth = table.shape[0]
        for i in range(images):
            patch = patches[pl.ds(me * images + i, 1), :rows]
            row = (patch * 4682) >> 16
            place = jnp.where(e < 2, row, patch - row * GRID)
            hot = jnp.where(iota((depth, rows), 0) == place, 1.0, 0.0).astype(BF16)
            placed = dot(jnp.concatenate([hot, hot, hot], 0), stacked, TN)
            x0[i * rows : (i + 1) * rows, d * narrow : (d + 1) * narrow] = (
                x_refs[d][i * rows : (i + 1) * rows, :].astype(F32) + placed
            )
    xhat, _ = norm_parts(x0[...])
    h1 = (xhat * vecs[0:1] + vecs[1:2]).astype(BF16)
    h1_out[...] = h1
    for z in range(parts):
        shift = g1[z * BLOCKS, narrow:, :].astype(F32)
        shift = jnp.concatenate([shift[6:7], shift[7:8, : wide - shift.shape[1]]], 1)
        qkv_out[z] = (dot(h1, wq[z], NN) + shift).astype(BF16)
    factor = HEAD_DIM ** (-0.5)
    for b in range(images):
        seen = iota((rows, rows), 1) < counts[me * images + b]
        span = slice(b * rows, (b + 1) * rows)
        for z in range(parts):
            mixed = []
            for i in range(heads):
                at = 3 * HEAD_DIM * i
                query = qkv_out[z, span, at : at + HEAD_DIM]
                key = qkv_out[z, span, at + HEAD_DIM : at + 2 * HEAD_DIM]
                value = qkv_out[z, span, at + 2 * HEAD_DIM : at + 3 * HEAD_DIM]
                scores = jnp.where(seen, dot(query, key, NT) * factor, NEGATIVE)
                weights = jnp.exp(scores - jnp.max(scores, 1, keepdims=True))
                chance = (weights / jnp.sum(weights, 1, keepdims=True)).astype(BF16)
                p_out[z * heads + i, b] = chance
                mixed.append(dot(chance, value, NN).astype(BF16))
            o_out[span, z * narrow : (z + 1) * narrow] = jnp.concatenate(mixed, 1)
    attn = dot(o_out[...], jnp.concatenate([wo[z] for z in range(parts)], 0), NN)
    x1_out[...] = x0[...] + attn + vecs[4:5]


def hidden_kernel(meta, *refs):
    x1, y_refs, (vecs, inb, g2, g3) = refs[0], refs[1:5], refs[5:9]
    d2, d3, dinb, out, dx1, da, vec_grads = refs[9:16]
    h2s, dys, y_total, dh_total = refs[16:]
    me = meta[0]
    parts, narrow = len(y_refs), y_refs[0].shape[1]
    step = pl.program_id(0)

    @pl.when(step == 0)
    def _():
        for d in range(parts):
            dys[:, d * narrow : (d + 1) * narrow] = y_refs[d][...]
        xhat, _ = norm_parts(x1[...])
        h2s[...] = (xhat * vecs[2:3] + vecs[3:4]).astype(BF16)
        y_total[...] = jnp.zeros_like(y_total)
        dh_total[...] = jnp.zeros_like(dh_total)

    w_in = jnp.concatenate([g2[me ^ d, 0] for d in range(parts)], 0)
    w_back = jnp.concatenate([g3[me ^ d, 0] for d in range(parts)], 0)
    h2 = h2s[...]
    dy = dys[...]
    hidden = dot(h2, w_in, NN) + inb[0]
    gate = 0.5 + 0.5 * lax.erf(hidden * (0.5**0.5))
    active = (hidden * gate).astype(BF16)
    slope = gate + hidden * jnp.exp(-0.5 * hidden * hidden) * 0.3989422804014327
    y_total[...] += dot(active, w_back, NT)
    grad_hidden = dot(dy, w_back, NN) * slope
    low = grad_hidden.astype(BF16)
    dinb[0] = colsum(low.astype(F32))
    dh_total[...] += dot(low, w_in, NT)
    d_back = dot(dy, active, TN)
    d_in = dot(h2, low, TN)
    for d in range(parts):
        d2[me ^ d, 0] = d_in[d * narrow : (d + 1) * narrow].astype(d2.dtype)
        d3[me ^ d, 0] = d_back[d * narrow : (d + 1) * narrow].astype(d3.dtype)

    @pl.when(step == pl.num_programs(0) - 1)
    def _():
        values = x1[...]
        result = (values + y_total[...] + vecs[5:6]).astype(BF16)
        for d in range(parts):
            out[d] = result[:, d * narrow : (d + 1) * narrow]
        xhat, factor = norm_parts(values)
        grad = dh_total[...]
        dy_wide = dys[...].astype(F32)
        total = dy_wide + norm_back(grad, xhat, factor, vecs[2:3])
        dx1[...] = total
        narrowed = total.astype(BF16)
        da[...] = narrowed
        vec_grads[0:1] = colsum(grad * xhat)
        vec_grads[1:2] = colsum(grad)
        vec_grads[2:3] = colsum(narrowed.astype(F32))
        vec_grads[3:4] = colsum(dy_wide)
        vec_grads[4:8] = jnp.zeros_like(vec_grads[4:8])


def attend_back_kernel(images, rows, da, o_ref, qkv, p_ref, wo, dqkv, dwo, dshift, do_ref):
    parts, narrow = wo.shape[0], wo.shape[1]
    heads = narrow // HEAD_DIM
    factor = HEAD_DIM ** (-0.5)
    grad = da[...]
    for z in range(parts):
        do_ref[z] = dot(grad, wo[z], NT).astype(BF16)
        dwo[z] = dot(o_ref[:, z * narrow : (z + 1) * narrow], grad, TN).astype(dwo.dtype)
    for b in range(images):
        span = slice(b * rows, (b + 1) * rows)
        for z in range(parts):
            grads = []
            for i in range(heads):
                at = 3 * HEAD_DIM * i
                query = qkv[z, span, at : at + HEAD_DIM]
                key = qkv[z, span, at + HEAD_DIM : at + 2 * HEAD_DIM]
                value = qkv[z, span, at + 2 * HEAD_DIM : at + 3 * HEAD_DIM]
                grad_head = do_ref[z, span, i * HEAD_DIM : (i + 1) * HEAD_DIM]
                low = p_ref[z * heads + i, b]
                chance = low.astype(F32)
                grad_chance = dot(grad_head, value, NT)
                inner = jnp.sum(chance * grad_chance, 1, keepdims=True)
                grad_score = (chance * (grad_chance - inner)).astype(BF16)
                grads.append((dot(grad_score, key, NN) * factor).astype(BF16))
                grads.append((dot(grad_score, query, TN) * factor).astype(BF16))
                grads.append(dot(low, grad_head, TN).astype(BF16))
            dqkv[z, span, :] = jnp.concatenate(grads, 1)
    for z in range(parts):
        dshift[z] = colsum(dqkv[z].astype(F32))


def last_kernel(meta, x0, h1, dqkv, wq, dx1, vecs, dwo, dshift, dinb, vec_grads, d1, gx, rows_ref):
    me = meta[0]
    parts, narrow = gx.shape[0], gx.shape[2]
    half = wq.shape[2] // 2
    outer = narrow // 2
    width = d1.shape[3]
    grad = dot(dqkv[0], wq[0], NT)
    for z in range(1, parts):
        grad += dot(dqkv[z], wq[z], NT)
    xhat, factor = norm_parts(x0[...])
    result = (dx1[...] + norm_back(grad, xhat, factor, vecs[0:1])).astype(BF16)
    rows_ref[0:1] = colsum(grad * xhat)
    rows_ref[1:2] = colsum(grad)
    rows_ref[2:6] = vec_grads[0:4]
    for d in range(parts):
        gx[d] = result[:, d * narrow : (d + 1) * narrow]
    feature = h1[...]
    for z in range(parts):
        dw = dot(feature, dqkv[z], TN).astype(d1.dtype)
        for d in range(parts):
            for k in range(2):
                d1[me ^ d, 2 * z + k, :narrow, :half] = dw[
                    d * narrow : (d + 1) * narrow, k * half : (k + 1) * half
                ]
                at = d * narrow + k * outer
                d1[z, 2 * (me ^ d) + k, :narrow, half:] = dwo[z, :, at : at + outer]
    gap = jnp.zeros((6, width - narrow), F32)
    for d in range(parts):
        shift = dshift[me ^ d]
        six = jnp.concatenate([rows_ref[0:6, d * narrow : (d + 1) * narrow], gap], 1)
        second = jnp.concatenate([shift[:, width:], gap[0:1, : 2 * width - 2 * half]], 1)
        for h in range(BLOCKS):
            tail = [six, shift[:, :width], second, dinb[h], jnp.zeros((7, width), F32)]
            d1[me ^ d, h, narrow:, :] = jnp.concatenate(tail, 0).astype(d1.dtype)


def call(kernel, outs, operands, scratch=(), name=None):
    specs = []
    values = []
    for value in operands:
        specs.append(SMEM if value.dtype == jnp.int32 and value.ndim == 1 else VMEM)
        values.append(value)
    return pl.pallas_call(
        kernel,
        out_shape=outs,
        in_specs=specs,
        out_specs=jax.tree.map(lambda _: VMEM, outs),
        scratch_shapes=scratch,
        compiler_params=PARAMS,
        name=name,
    )(*values)


def shaped(dtype, *shape):
    return jax.ShapeDtypeStruct(shape, dtype)


def exchange(block, d):
    size = lax.axis_size("ea")
    return block if d == 0 else lax.ppermute(block, "ea", [(e, e ^ d) for e in range(size)])


def vector_rows(vectors, shift, bias):
    width = bias.shape[-1]
    rows = [jnp.pad(v, (0, width - v.shape[0])) for v in vectors]
    rows += [shift[:width], jnp.pad(shift[width:], (0, 2 * width - shift.shape[0])), bias]
    return jnp.stack(rows + [jnp.zeros_like(bias)] * (VEC_ROWS - len(rows)))


def shards(
    tokens,
    image_counts,
    kept_patches,
    norm1_gain,
    norm1_bias,
    qkv_weight,
    query_bias,
    value_bias,
    out_weight,
    out_bias,
    norm2_gain,
    norm2_bias,
    in_weight,
    in_bias,
    back_weight,
    back_bias,
    cotangent,
):
    parts = lax.axis_size("ea")
    columns = lax.axis_size("ha")
    me = lax.axis_index("ea")
    mine = lax.axis_index("ha")
    meta = jnp.stack([me, mine]).astype(jnp.int32)
    narrow, slots = tokens.shape
    full = narrow * parts
    images = image_counts.shape[0] // parts
    most = kept_patches.shape[1]
    rows = -(-most // 16) * 16
    count = images * rows
    window = min(slots, (images * most + 127 + 127) // 128 * 128)
    heads = full // HEAD_DIM
    group_heads = narrow // HEAD_DIM
    hidden_block = in_weight.shape[1] * columns // BLOCKS
    half = 3 * narrow // 2

    pairs = jnp.zeros((group_heads, HEAD_DIM), BF16)
    shift = jnp.stack(
        [query_bias.reshape(group_heads, HEAD_DIM), pairs, value_bias.reshape(group_heads, HEAD_DIM)],
        1,
    ).reshape(-1)
    vectors = (norm1_gain, norm1_bias, norm2_gain, norm2_bias, out_bias, back_bias)
    back_turned = back_weight.T
    if columns == BLOCKS:
        below = vector_rows(vectors, shift, in_bias)
        first = jnp.concatenate([jnp.concatenate([qkv_weight, out_weight], 1), below], 0)
        g1 = lax.all_gather(first, ("ea", "ha"))
        g2 = lax.all_gather(in_weight, ("ea", "ha"))
        g3 = lax.all_gather(back_turned, ("ea", "ha"))
    else:

        def whole(weight):
            wide = lax.all_gather(weight, "ha", axis=1, tiled=True)
            blocks = wide.reshape(narrow, BLOCKS, -1).transpose(1, 0, 2)
            return lax.all_gather(blocks, "ea")

        biases = lax.all_gather(in_bias, "ha", tiled=True).reshape(BLOCKS, -1)
        below = jax.vmap(lambda bias: vector_rows(vectors, shift, bias))(biases)
        g1 = jnp.concatenate([whole(qkv_weight), whole(out_weight)], 3)
        g1 = jnp.concatenate([g1, lax.all_gather(below, "ea")], 2)
        g2 = whole(in_weight)
        g3 = whole(back_turned)
        g1 = g1.reshape(parts * BLOCKS, narrow + VEC_ROWS, hidden_block)
    g2 = g2.reshape(parts, BLOCKS, narrow, hidden_block)
    g3 = g3.reshape(parts, BLOCKS, narrow, hidden_block)

    x_packed, y_packed = call(
        partial(pack_kernel, images, rows, window),
        (shaped(BF16, parts, count, narrow),) * 2,
        (meta, image_counts, tokens, cotangent),
        (pltpu.SMEM((image_counts.shape[0],), jnp.int32), pltpu.VMEM((count, window), BF16)),
        "pack",
    )
    xs = [exchange(x_packed[d], d) for d in range(parts)]
    ys = [exchange(y_packed[d], d) for d in range(parts)]

    omega = 1.0 / 10000.0 ** (jnp.arange(narrow, dtype=F32) / narrow)
    angles = jnp.arange(16, dtype=F32)[:, None] * omega[None, :]
    patches = jnp.pad(kept_patches, ((0, 0), (0, 128 - most)))

    x1, x0, h1, qkv, chances, mixed, vecs, inb, wq, wo = call(
        partial(attend_kernel, images, rows),
        (
            shaped(F32, count, full),
            shaped(F32, count, full),
            shaped(BF16, count, full),
            shaped(BF16, parts, count, 3 * narrow),
            shaped(BF16, heads, images, rows, rows),
            shaped(BF16, count, full),
            shaped(F32, VEC_ROWS, full),
            shaped(F32, BLOCKS, 1, hidden_block),
            shaped(BF16, parts, full, 3 * narrow),
            shaped(BF16, parts, narrow, full),
        ),
        (meta, image_counts, *xs, patches, jnp.sin(angles), jnp.cos(angles), g1),
        name="attend",
    )

    whole_spec = lambda *shape: pl.BlockSpec(shape, lambda h: (0,) * len(shape))
    block_spec = pl.BlockSpec((parts, 1, narrow, hidden_block), lambda h: (0, h, 0, 0))
    bias_spec = pl.BlockSpec((1, 1, hidden_block), lambda h: (h, 0, 0))
    d2, d3, dinb, outs, dx1, da, vec_grads = pl.pallas_call(
        hidden_kernel,
        grid=(BLOCKS,),
        out_shape=(
            shaped(BF16, parts, BLOCKS, narrow, hidden_block),
            shaped(BF16, parts, BLOCKS, narrow, hidden_block),
            shaped(F32, BLOCKS, 1, hidden_block),
            shaped(BF16, parts, count, narrow),
            shaped(F32, count, full),
            shaped(BF16, count, full),
            shaped(F32, 8, full),
        ),
        in_specs=[SMEM, whole_spec(count, full)]
        + [whole_spec(count, narrow)] * parts
        + [whole_spec(VEC_ROWS, full), bias_spec, block_spec, block_spec],
        out_specs=(
            block_spec,
            block_spec,
            bias_spec,
            whole_spec(parts, count, narrow),
            whole_spec(count, full),
            whole_spec(count, full),
            whole_spec(8, full),
        ),
        scratch_shapes=(
            pltpu.VMEM((count, full), BF16),
            pltpu.VMEM((count, full), BF16),
            pltpu.VMEM((count, full), F32),
            pltpu.VMEM((count, full), F32),
        ),
        compiler_params=PARAMS,
        name="hidden",
    )(meta, x1, *ys, vecs, inb, g2, g3)

    dqkv, dwo, dshift = call(
        partial(attend_back_kernel, images, rows),
        (
            shaped(BF16, parts, count, 3 * narrow),
            shaped(BF16, parts, narrow, full),
            shaped(F32, parts, 1, 3 * narrow),
        ),
        (da, mixed, qkv, chances, wo),
        (pltpu.VMEM((parts, count, narrow), BF16),),
        "attend_back",
    )
    d1, gx = call(
        last_kernel,
        (
            shaped(BF16, parts, BLOCKS, narrow + VEC_ROWS, hidden_block),
            shaped(BF16, parts, count, narrow),
        ),
        (meta, x0, h1, dqkv, wq, dx1, vecs, dwo, dshift, dinb, vec_grads),
        (pltpu.VMEM((8, full), F32),),
        "last",
    )

    def unpack(blocks, dtype):
        return call(
            partial(unpack_kernel, images, rows, window),
            shaped(dtype, narrow, slots),
            (meta, image_counts, *[exchange(blocks[d], d) for d in range(parts)]),
            (
                pltpu.SMEM((image_counts.shape[0],), jnp.int32),
                pltpu.VMEM((count, window), BF16),
                pltpu.VMEM((narrow, slots), F32),
            ),
            "unpack",
        )

    output = unpack(outs, BF16)
    grad_tokens = unpack(gx, F32)

    if columns == BLOCKS:

        def scatter(blocks):
            flat = blocks.reshape(parts * BLOCKS, *blocks.shape[2:])
            return lax.psum_scatter(flat, ("ea", "ha")).astype(F32)

        s1, grad_in, grad_back = scatter(d1), scatter(d2), scatter(d3)
        grad_qkv, grad_out, small = s1[:narrow, :half], s1[:narrow, half:], s1[narrow:]
        grad_in_bias = small[8]
    else:

        def scatter(blocks):
            mixed_blocks = lax.psum_scatter(blocks.astype(F32), "ea")
            flat = mixed_blocks.transpose(1, 0, 2).reshape(narrow, -1)
            return lax.psum_scatter(flat, "ha", scatter_dimension=1, tiled=True)

        grad_in, grad_back = scatter(d2), scatter(d3)
        grad_qkv, grad_out = scatter(d1[:, :, :narrow, :half]), scatter(d1[:, :, :narrow, half:])
        small = lax.psum(d1[:, :, narrow:].astype(F32), ("ea", "ha"))
        size = in_bias.shape[0]
        grad_in_bias = lax.dynamic_slice_in_dim(small[0, :, 8].reshape(-1), mine * size, size, 0)
        small = lax.dynamic_index_in_dim(small[:, 0], me, 0, False)
    small_shift = jnp.concatenate([small[6], small[7]])[: 3 * narrow]
    small_shift = small_shift.reshape(group_heads, 3, HEAD_DIM)
    return (
        output,
        grad_tokens,
        small[0, :narrow],
        small[1, :narrow],
        grad_qkv,
        small_shift[:, 0].reshape(-1),
        small_shift[:, 2].reshape(-1),
        grad_out,
        small[4, :narrow],
        small[2, :narrow],
        small[3, :narrow],
        grad_in,
        grad_in_bias,
        grad_back.T,
        small[5, :narrow],
    )


def solution(mesh):
    return jax.shard_map(
        shards,
        mesh=mesh,
        in_specs=(
            P("ea", "ha"),
            P("ha"),
            P("ha", None),
            P("ea"),
            P("ea"),
            P("ea", "ha"),
            P("ea"),
            P("ea"),
            P("ea", "ha"),
            P("ea"),
            P("ea"),
            P("ea"),
            P("ea", "ha"),
            P("ha"),
            P("ha", "ea"),
            P("ea"),
            P("ea", "ha"),
        ),
        out_specs=(
            P("ea", "ha"),
            P("ea", "ha"),
            P("ea"),
            P("ea"),
            P("ea", "ha"),
            P("ea"),
            P("ea"),
            P("ea", "ha"),
            P("ea"),
            P("ea"),
            P("ea"),
            P("ea", "ha"),
            P("ha"),
            P("ha", "ea"),
            P("ea"),
        ),
        check_vma=False,
    )
```

time: 1060 us -> 603 us (0.57)
  waiting for transfers between devices: 659 us -> 456 us
  matrix products: 142 us -> 0 us
  blocking collectives: 139 us -> 0 us
  Pallas kernels: 0 us -> 88.5 us
  other arithmetic: 78 us -> 6.63 us
  starting transfers between devices: 1.39 us -> 17.7 us
    all_gather x6 -> x3, waiting for transfers between devices: 304 us -> 160 us  [the longest x1 65.5 us: shards(): g3 = lax.all_gather(back_turned, ('ea', 'ha'))]
    dot_general x28 -> x0, matrix products: 132 us -> none  [the longest x3 12.3 us: shards(): lax.dot_general(grad_score, query, OVER_ROWS, preferred_element_type=jnp....]
    psum x5 -> x0, blocking collectives: 90.5 us -> none  [the longest x4 73.3 us: row_totals(): return lax.psum((jnp.sum(first_term, 1), jnp.sum(second_term, 1)), 'ea')]
    pallas_call x0 -> x7, Pallas kernels: none -> 88.5 us  [the longest x6 60.3 us: call(): pl.pallas_call(kernel, out_shape=outs, in_specs=specs, out_specs=jax.tree...]
    reduce_scatter x6 -> x3, waiting for transfers between devices: 354 us -> 266 us  [scatter(): return lax.psum_scatter(flat, ('ea', 'ha')).astype(F32)]
    all_gather x3 -> x0, blocking collectives: 48.2 us -> none  [the longest x1 19.3 us: shards(): lax.all_gather(qkv_weight, 'ha', axis=1, tiled=True)]
    convert_element_type x15 -> x2, other arithmetic: 36.3 us -> 2.6 us  [scatter(): return lax.psum_scatter(flat, ('ea', 'ha')).astype(F32)]
    reduce_sum x11 -> x0, other arithmetic: 27.9 us -> none  [the longest x3 14.4 us: shards(): jnp.sum(jnp.exp(scores - peak_score), 1, keepdims=True)]
  transfers between devices with their start and end apart: 15 -> 18, of which waited for: 9 -> 13; matrix products, arithmetic and copies ran while one was open for 12% -> 2% of each run, Pallas kernels for 0% -> 10%
where the time goes in v1:
time: 603 us
  waiting for transfers between devices  456 us (76%)
  Pallas kernels  88.5 us (15%)
  local copies, waits for them, and re-layouts  20.2 us (3%)
  starting transfers between devices  17.7 us (3%)
  between operations  14.3 us (2%)
  other arithmetic  6.63 us (1%)
    reduce_scatter x3, waiting for transfers between devices, scatter(): return lax.psum_scatter(flat, ('ea', 'ha')).astype(F32)  266 us
    all_gather x1, waiting for transfers between devices, shards(): g3 = lax.all_gather(back_turned, ('ea', 'ha'))  65.5 us
    pallas_call x6, Pallas kernels, call(): pl.pallas_call(kernel, out_shape=outs, in_specs=specs, out_specs=jax.tree...  60.3 us
    all_gather x1, waiting for transfers between devices, shards(): g2 = lax.all_gather(in_weight, ('ea', 'ha'))  49.3 us
    all_gather x1, waiting for transfers between devices, shards(): g1 = lax.all_gather(first, ('ea', 'ha'))  45 us
    pallas_call x1, Pallas kernels, shards(): pl.pallas_call(hidden_kernel, grid=(BLOCKS,), out_shape=(shaped(BF16, par...  28.3 us
    ppermute x12, waiting for transfers between devices, exchange(): lax.ppermute(block, 'ea', [(e, e ^ d) for e in range(size)])  27.5 us
    ppermute x12, starting transfers between devices, exchange(): lax.ppermute(block, 'ea', [(e, e ^ d) for e in range(size)])  17.4 us
  transfers between devices with their start and end apart: 18, of which 13 were waited for; matrix products, arithmetic and copies ran while one was open for 2% of the time, Pallas kernels for 10%

profile of v1, /device:TPU:0, one launch (start us, length us, event | category | flops | bytes accessed | tf_op | source)
XLA Modules:
  0.0 602.8 jit_solution(8669230811579307490)
XLA Ops:
  7.2 0.7 stack_reshape.6
  8.0 0.7 stack_reshape.7
  8.9 0.7 pad.27
  9.6 0.7 pad.28
  10.4 0.7 pad.31
  11.1 0.7 pad.29
  11.8 0.7 pad.30
  12.4 0.7 pad.32
  13.1 0.7 stack.51
  13.8 1.0 pad_maximum_fusion
  14.8 1.9 concatenate.23
  16.9 0.7 all-gather.9.cloned.1.call-update
  17.6 0.7 all-gather.11.cloned.1.call-update
  18.3 0.6 pad_add_fusion.meta
  18.9 4.3 pack.1
  23.2 2.1 slice_bitcast_fusion.12
  25.3 3.9 collective-permute-start.2
  29.2 0.5 collective-permute-start.1
  29.8 0.8 slice_bitcast_fusion.8
  30.5 2.9 collective-permute-start.5
  33.5 0.5 collective-permute-start.4
  34.0 0.6 pad.26.refs_4_
  34.6 2.2 collective-permute-done.2.refs_3_
  36.8 1.8 collective-permute-start.3
  38.5 0.7 fusion
  39.2 6.0 collective-permute-done.1.refs_2_
  45.2 45.0 %all-gather.7.cloned.1.call-done = bf16[6656,384]{1,0:T(8,128)(2,1)} async-done(((bf16[208,384]{1,0:T(8,128)(2,1)}), bf16[6656,384]{1,0:T(8,128)(2,1)}) %all-gather.7.cloned.1.call-update) | async-done | bytes 5111824 | tf_op jit(solution)/shard_map/all_gather | solution.py:363
  90.2 16.2 %attend.1 = (f32[448,768]{1,0:T(8,128)}, f32[448,768]{1,0:T(8,128)}, bf16[448,768]{1,0:T(8,128)(2,1)}, bf16[4,448,576]{2,1,0:T(8,128)(2,1)}, bf16[12,4,112,112]{...) custom-call(s32[2]{0:T(128)} %pad_add_fusion.meta, ...), custom_call_target="tpu_custom_call" | custom-call | tf_op jit(solution)/shard_map/attend/pallas_call | solution.py:290
  106.4 49.3 %all-gather.9.cloned.1.call-done = bf16[6144,384]{1,0:T(8,128)(2,1)} async-done(((bf16[192,384]{1,0:T(8,128)(2,1)}), bf16[6144,384]{1,0:T(8,128)(2,1)}) %all-gather.9.cloned.1.call-update) | async-done | bytes 4718608 | tf_op jit(solution)/shard_map/all_gather | solution.py:364
  155.8 65.5 %all-gather.11.cloned.1.call-done = bf16[6144,384]{1,0:T(8,128)(2,1)} async-done(((bf16[192,384]{1,0:T(8,128)(2,1)}), bf16[6144,384]{1,0:T(8,128)(2,1)}) %all-gather.11.cloned.1.call-update) | async-done | bytes 4718608 | tf_op jit(solution)/shard_map/all_gather | solution.py:365
  221.3 28.3 %hidden.1 = (bf16[4,8,192,384]{3,2,1,0:T(8,128)(2,1)}, bf16[4,8,192,384]{3,2,1,0:T(8,128)(2,1)}, f32[8,1,384]{2,1,0:T(1,128)}, bf16[4,448,192]{2,1,0:T(8,128)(2,...) custom-call(s32[2]{0:T(128)} %pad_add_fusion.meta, f32[448,768]{1,0:T(8,128)} %get-tuple-element.40.refs_0_, ...), custom_call_target="tpu_custom_call" | custom-call | tf_op jit(solution)/shard_map/hidden/pallas_call | solution.py:418
  249.7 0.5 reduce-scatter.6.cloned.1.call-update
  250.3 20.3 %attend_back.1 = (bf16[4,448,576]{2,1,0:T(8,128)(2,1)}, bf16[4,192,768]{2,1,0:T(8,128)(2,1)}, f32[4,1,576]{2,1,0:T(1,128)}) custom-call(bf16[448,768]{1,0:T(8,128)(2,1)} %get-tuple-element.47.da, bf16[448,768]{1,0:T(8,128)(2,1)} %get-tuple-element.48.o_ref, bf16[4,448,576]{2,1,0:T(8,128)(2,1)} %get-tuple-element.49.qkv, ...), custom_call_target="tpu_custom_call" | custom-call | tf_op jit(solution)/shard_map/attend_back/pallas_call | solution.py:290
  270.5 12.8 %last.1 = (bf16[4,8,208,384]{3,2,1,0:T(8,128)(2,1)}, bf16[4,448,192]{2,1,0:T(8,128)(2,1)}) custom-call(s32[2]{0:T(128)} %pad_add_fusion.meta, f32[448,768]{1,0:T(8,128)} %get-tuple-element.45.x0, bf16[448,768]{1,0:T(8,128)(2,1)} %get-tuple-element.46.h1, bf16[4,448,576]{2,1,0:T(8,128)(2,1)} %get-tuple-element.52.dqkv, ...), custom_call_target="tpu_custom_call" | custom-call | tf_op jit(solution)/shard_map/last/pallas_call | solution.py:290
  283.4 1.2 copy-done
  284.5 0.7 slice_bitcast_fusion.4
  285.3 1.5 collective-permute-start.8
  286.8 1.4 collective-permute-start.7
  288.2 0.6 collective-permute-start.6
  288.8 0.7 slice_bitcast_fusion
  289.5 1.5 collective-permute-start.11
  291.0 1.4 collective-permute-start.10
  292.4 2.2 collective-permute-done.8.refs_3_
  294.7 1.4 collective-permute-start.9
  296.1 3.5 collective-permute-done.7.refs_2_
  299.6 0.7 copy-done.11
  300.4 3.3 unpack.2
  303.7 4.7 collective-permute-done.11.refs_3_
  308.4 5.1 collective-permute-done.10.refs_2_
  313.5 3.7 collective-permute-done.9.refs_1_
  317.2 0.7 copy-done.14
  317.9 3.5 unpack.3
  321.4 43.7 %reduce-scatter.8.cloned.1.call-done = bf16[1,192,384]{2,1,0:T(8,128)(2,1)} async-done(((bf16[32,192,384]{2,1,0:T(8,128)(2,1)}), bf16[1,192,384]{2,1,0:T(8,128)(2,1)}) %reduce-scatter.8.cloned.1.call-update) | async-done | bytes 147472 | tf_op jit(solution)/shard_map/reduce_scatter | solution.py:494
  365.1 1.6 convert_bitcast_fusion
  366.7 110.7 %reduce-scatter.6.cloned.1.call-done = bf16[1,192,384]{2,1,0:T(8,128)(2,1)} async-done(((bf16[32,192,384]{2,1,0:T(8,128)(2,1)}), bf16[1,192,384]{2,1,0:T(8,128)(2,1)}) %reduce-scatter.6.cloned.1.call-update) | async-done | bytes 147472 | tf_op jit(solution)/shard_map/reduce_scatter | solution.py:494
  477.4 1.6 bitcast_convert_fusion
  479.1 111.8 %reduce-scatter.4.cloned.1.call-done = bf16[1,208,384]{2,1,0:T(8,128)(2,1)} async-done(((bf16[32,208,384]{2,1,0:T(8,128)(2,1)}), bf16[1,208,384]{2,1,0:T(8,128)(2,1)}) %reduce-scatter.4.cloned.1.call-update) | async-done | bytes 159760 | tf_op jit(solution)/shard_map/reduce_scatter | solution.py:494
  590.8 1.0 fusion.3
  591.8 0.6 fusion.2
  592.4 0.7 slice.155
  593.1 0.7 slice.150
  593.9 0.6 slice_reduce_fusion
  594.7 0.6 reshape_squeeze.7
  595.3 0.6 reshape_squeeze.6
  (68 shorter events, 1.1 us)
Async XLA Ops:
  7.2 83.0 %all-gather.7.cloned.1.call-start = ((), (), s32[]{:S(2)}) async-start(), calls=%async_computation.6 | async-start | bytes 5271552 | tf_op jit(solution)/shard_map/all_gather | solution.py:363
  16.8 139.0 %all-gather.9.cloned.1.call-start = ((), (), s32[]{:S(2)}) async-start(), calls=%async_computation.7 | async-start | bytes 4866048 | tf_op jit(solution)/shard_map/all_gather | solution.py:364
  17.6 203.8 %all-gather.11.cloned.1.call-start = ((), (), s32[]{:S(2)}) async-start(), calls=%async_computation.8 | async-start | bytes 4866048 | tf_op jit(solution)/shard_map/all_gather | solution.py:365
  18.3 346.8 %reduce-scatter.8.cloned.1.call-start = ((), (), s32[]{:S(2)}) async-start(), calls=%async_computation.5 | async-start | bytes 4866048 | tf_op jit(solution)/shard_map/reduce_scatter | solution.py:494
  18.9 15.0 %copy-start.15 = (s32[16,98]{1,0:T(8,128)S(1)}, s32[16,98]{1,0:T(8,128)}, u32[]{:S(2)}) copy-start(s32[16,98]{1,0:T(8,128)} %param.19) | copy-start | bytes 18820
  23.2 6.6 %copy-start.2 = (bf16[4,448,192]{2,1,0:T(8,128)(2,1)S(1)}, bf16[4,448,192]{2,1,0:T(8,128)(2,1)}, u32[]{:S(2)}) copy-start(bf16[4,448,192]{2,1,0:T(8,128)(2,1)} %get-tuple-element.41) | copy-start | bytes 2064388
  25.3 11.5 %collective-permute-start.2 = (bf16[448,192]{1,0:T(8,128)(2,1)S(1)}, bf16[448,192]{1,0:T(8,128)(2,1)S(1)}, u32[]{:S(2)}, u32[]{:S(2)}) collective-permute-start(bf16[448,192]{1,0:T(8,128)(2,1)S(1)} %get-tuple-element.80), channel_id=1, source_target_pairs={{0,24},{8,16},{16,8},{24,0},{1,25},{9,17},{17,9},{25,1},{2,26},{10... | collective-permute-start | bytes 516104 | tf_op jit(solution)/shard_map/ppermute | solution.py:307
  29.2 16.0 %collective-permute-start.1 = (bf16[448,192]{1,0:T(8,128)(2,1)S(1)}, bf16[448,192]{1,0:T(8,128)(2,1)S(1)}, u32[]{:S(2)}, u32[]{:S(2)}) collective-permute-start(bf16[448,192]{1,0:T(8,128)(2,1)S(1)} %get-tuple-element.81), channel_id=1, source_target_pairs={{0,16},{8,24},{16,0},{24,8},{1,17},{9,25},{17,1},{25,9},{2,18},{10... | collective-permute-start | bytes 516104 | tf_op jit(solution)/shard_map/ppermute | solution.py:307
  29.7 15.5 %collective-permute-start = (bf16[448,192]{1,0:T(8,128)(2,1)S(1)}, bf16[448,192]{1,0:T(8,128)(2,1)S(1)}, u32[]{:S(2)}, u32[]{:S(2)}) collective-permute-start(bf16[448,192]{1,0:T(8,128)(2,1)S(1)} %get-tuple-element.82), channel_id=1, source_target_pairs={{0,8},{8,0},{16,24},{24,16},{1,9},{9,1},{17,25},{25,17},{2,10},{10... | collective-permute-start | bytes 516104 | tf_op jit(solution)/shard_map/ppermute | solution.py:307
  30.5 75.8 %collective-permute-start.5 = (bf16[448,192]{1,0:T(8,128)(2,1)S(1)}, bf16[448,192]{1,0:T(8,128)(2,1)S(1)}, u32[]{:S(2)}, u32[]{:S(2)}) collective-permute-start(bf16[448,192]{1,0:T(8,128)(2,1)S(1)} %get-tuple-element.76), channel_id=1, source_target_pairs={{0,24},{8,16},{16,8},{24,0},{1,25},{9,17},{17,9},{25,1},{2,26},{10... | collective-permute-start | bytes 516104 | tf_op jit(solution)/shard_map/ppermute | solution.py:307
  33.5 72.9 %collective-permute-start.4 = (bf16[448,192]{1,0:T(8,128)(2,1)S(1)}, bf16[448,192]{1,0:T(8,128)(2,1)S(1)}, u32[]{:S(2)}, u32[]{:S(2)}) collective-permute-start(bf16[448,192]{1,0:T(8,128)(2,1)S(1)} %get-tuple-element.77), channel_id=1, source_target_pairs={{0,16},{8,24},{16,0},{24,8},{1,17},{9,25},{17,1},{25,9},{2,18},{10... | collective-permute-start | bytes 516104 | tf_op jit(solution)/shard_map/ppermute | solution.py:307
  36.8 53.4 %copy-start.6 = (bf16[448,192]{1,0:T(8,128)(2,1)}, bf16[448,192]{1,0:T(8,128)(2,1)S(1)}, u32[]{:S(2)}) copy-start(bf16[448,192]{1,0:T(8,128)(2,1)S(1)} %collective-permute-done.2.refs_3_) | copy-start | bytes 516100
  36.8 69.6 %collective-permute-start.3 = (bf16[448,192]{1,0:T(8,128)(2,1)S(1)}, bf16[448,192]{1,0:T(8,128)(2,1)S(1)}, u32[]{:S(2)}, u32[]{:S(2)}) collective-permute-start(bf16[448,192]{1,0:T(8,128)(2,1)S(1)} %get-tuple-element.78), channel_id=1, source_target_pairs={{0,8},{8,0},{16,24},{24,16},{1,9},{9,1},{17,25},{25,17},{2,10},{10... | collective-permute-start | bytes 516104 | tf_op jit(solution)/shard_map/ppermute | solution.py:307
  45.2 45.0 %copy-start.7 = (bf16[448,192]{1,0:T(8,128)(2,1)}, bf16[448,192]{1,0:T(8,128)(2,1)S(1)}, u32[]{:S(2)}) copy-start(bf16[448,192]{1,0:T(8,128)(2,1)S(1)} %collective-permute-done.1.refs_2_) | copy-start | bytes 516100
  45.2 45.0 %copy-start.8 = (bf16[448,192]{1,0:T(8,128)(2,1)}, bf16[448,192]{1,0:T(8,128)(2,1)S(1)}, u32[]{:S(2)}) copy-start(bf16[448,192]{1,0:T(8,128)(2,1)S(1)} %collective-permute-done.refs_1_) | copy-start | bytes 516100
  106.4 114.9 %copy-start.3 = (bf16[448,192]{1,0:T(8,128)(2,1)}, bf16[448,192]{1,0:T(8,128)(2,1)S(1)}, u32[]{:S(2)}) copy-start(bf16[448,192]{1,0:T(8,128)(2,1)S(1)} %collective-permute-done.5.refs_4_) | copy-start | bytes 516100
  106.4 114.9 %copy-start.4 = (bf16[448,192]{1,0:T(8,128)(2,1)}, bf16[448,192]{1,0:T(8,128)(2,1)S(1)}, u32[]{:S(2)}) copy-start(bf16[448,192]{1,0:T(8,128)(2,1)S(1)} %collective-permute-done.4.refs_3_) | copy-start | bytes 516100
  106.4 114.9 %copy-start.5 = (bf16[448,192]{1,0:T(8,128)(2,1)}, bf16[448,192]{1,0:T(8,128)(2,1)S(1)}, u32[]{:S(2)}) copy-start(bf16[448,192]{1,0:T(8,128)(2,1)S(1)} %collective-permute-done.3.refs_2_) | copy-start | bytes 516100
  249.6 227.8 %reduce-scatter.6.cloned.1.call-start = ((), (), s32[]{:S(2)}) async-start(), calls=%async_computation.4 | async-start | bytes 4866048 | tf_op jit(solution)/shard_map/reduce_scatter | solution.py:494
  250.2 340.6 %reduce-scatter.4.cloned.1.call-start = ((), (), s32[]{:S(2)}) async-start(), calls=%async_computation.3 | async-start | bytes 5271552 | tf_op jit(solution)/shard_map/reduce_scatter | solution.py:494
  283.3 1.2 copy-start
  283.3 5.4 copy-start.1
  285.3 9.4 %collective-permute-start.8 = (bf16[448,192]{1,0:T(8,128)(2,1)S(1)}, bf16[448,192]{1,0:T(8,128)(2,1)S(1)}, u32[]{:S(2)}, u32[]{:S(2)}) collective-permute-start(bf16[448,192]{1,0:T(8,128)(2,1)S(1)} %get-tuple-element.72), channel_id=1, source_target_pairs={{0,24},{8,16},{16,8},{24,0},{1,25},{9,17},{17,9},{25,1},{2,26},{10... | collective-permute-start | bytes 516104 | tf_op jit(solution)/shard_map/ppermute | solution.py:307
  286.8 12.9 %collective-permute-start.7 = (bf16[448,192]{1,0:T(8,128)(2,1)S(1)}, bf16[448,192]{1,0:T(8,128)(2,1)S(1)}, u32[]{:S(2)}, u32[]{:S(2)}) collective-permute-start(bf16[448,192]{1,0:T(8,128)(2,1)S(1)} %get-tuple-element.73), channel_id=1, source_target_pairs={{0,16},{8,24},{16,0},{24,8},{1,17},{9,25},{17,1},{25,9},{2,18},{10... | collective-permute-start | bytes 516104 | tf_op jit(solution)/shard_map/ppermute | solution.py:307
  288.2 11.5 %collective-permute-start.6 = (bf16[448,192]{1,0:T(8,128)(2,1)S(1)}, bf16[448,192]{1,0:T(8,128)(2,1)S(1)}, u32[]{:S(2)}, u32[]{:S(2)}) collective-permute-start(bf16[448,192]{1,0:T(8,128)(2,1)S(1)} %get-tuple-element.74), channel_id=1, source_target_pairs={{0,8},{8,0},{16,24},{24,16},{1,9},{9,1},{17,25},{25,17},{2,10},{10... | collective-permute-start | bytes 516104 | tf_op jit(solution)/shard_map/ppermute | solution.py:307
  289.5 18.8 %collective-permute-start.11 = (bf16[448,192]{1,0:T(8,128)(2,1)S(1)}, bf16[448,192]{1,0:T(8,128)(2,1)S(1)}, u32[]{:S(2)}, u32[]{:S(2)}) collective-permute-start(bf16[448,192]{1,0:T(8,128)(2,1)S(1)} %get-tuple-element.68), channel_id=1, source_target_pairs={{0,24},{8,16},{16,8},{24,0},{1,25},{9,17},{17,9},{25,1},{2,26},{10... | collective-permute-start | bytes 516104 | tf_op jit(solution)/shard_map/ppermute | solution.py:307
  291.0 22.5 %collective-permute-start.10 = (bf16[448,192]{1,0:T(8,128)(2,1)S(1)}, bf16[448,192]{1,0:T(8,128)(2,1)S(1)}, u32[]{:S(2)}, u32[]{:S(2)}) collective-permute-start(bf16[448,192]{1,0:T(8,128)(2,1)S(1)} %get-tuple-element.69), channel_id=1, source_target_pairs={{0,16},{8,24},{16,0},{24,8},{1,17},{9,25},{17,1},{25,9},{2,18},{10... | collective-permute-start | bytes 516104 | tf_op jit(solution)/shard_map/ppermute | solution.py:307
  294.7 5.0 copy-start.9
  294.7 22.5 %collective-permute-start.9 = (bf16[448,192]{1,0:T(8,128)(2,1)S(1)}, bf16[448,192]{1,0:T(8,128)(2,1)S(1)}, u32[]{:S(2)}, u32[]{:S(2)}) collective-permute-start(bf16[448,192]{1,0:T(8,128)(2,1)S(1)} %get-tuple-element.70), channel_id=1, source_target_pairs={{0,8},{8,0},{16,24},{24,16},{1,9},{9,1},{17,25},{25,17},{2,10},{10... | collective-permute-start | bytes 516104 | tf_op jit(solution)/shard_map/ppermute | solution.py:307
  299.6 0.7 copy-start.11
  299.6 0.8 copy-start.13
  308.4 8.8 %copy-start.10 = (bf16[448,192]{1,0:T(8,128)(2,1)}, bf16[448,192]{1,0:T(8,128)(2,1)S(1)}, u32[]{:S(2)}) copy-start(bf16[448,192]{1,0:T(8,128)(2,1)S(1)} %collective-permute-done.11.refs_3_) | copy-start | bytes 516100
  313.5 3.7 copy-start.12
  317.2 0.7 copy-start.14
Sparse Core Ops, SparseCore 0:
  16.9 73.2 all-gather.6
  93.2 62.5 all-gather.8
  158.8 62.4 all-gather.10
  249.7 115.3 reduce-scatter.7
  371.3 106.0 reduce-scatter.5
  482.8 107.9 reduce-scatter.3
